TPU v7x, 32 devices: a whole 2x2x4 slice. The times are simulated.
32 devices in a mesh: seq: 8 (over z, x), tp: 4 (over y, core).
Axes of the slice: x: 2, y: 2, z: 4, core: 2. Of those that a mesh axis runs over, the one named last changes fastest.
Arguments:
- hidden_in: bfloat16 [16, 2048], replicated, may hold values from -6 to 6
- lengths: int32 [16], replicated, may hold values from 1 to 511, 2431 in all
- positions: int32 [16], replicated, may hold values from 0 to 1023
- query_weight: bfloat16 [2, 2048, 2048], P(None, 'seq', 'tp'), may hold values from -0.125 to 0.125
- key_weight: bfloat16 [2, 2048, 512], P(None, 'seq', 'tp'), may hold values from -4 to 4
- value_weight: bfloat16 [2, 2048, 512], P(None, 'seq', 'tp'), may hold values from -0.125 to 0.125
- out_weight: bfloat16 [2, 2048, 2048], P(None, 'tp', 'seq'), may hold values from -0.125 to 0.125
- gate_weight: bfloat16 [2, 2048, 8192], P(None, 'seq', 'tp'), may hold values from -0.125 to 0.125
- up_weight: bfloat16 [2, 2048, 8192], P(None, 'seq', 'tp'), may hold values from -0.125 to 0.125
- down_weight: bfloat16 [2, 8192, 2048], P(None, 'tp', 'seq'), may hold values from -0.0625 to 0.0625
- key_cache: bfloat16 [2, 16, 512, 512], P(None, None, 'seq', 'tp'), may hold values from -80 to 80
- value_cache: bfloat16 [2, 16, 512, 512], P(None, None, 'seq', 'tp'), may hold values from -6 to 6
Outputs:
- hidden_out: bfloat16 [16, 2048], replicated
- key_out: bfloat16 [2, 16, 512, 512], P(None, None, 'seq', 'tp')
- value_out: bfloat16 [2, 16, 512, 512], P(None, None, 'seq', 'tp')
Inputs may be any that keep to these rules, and one draw needn't show every extreme that they name: Request b has its cached rows at positions 0 .. lengths[b] - 1 and its new token goes to row lengths[b]; rows above are padding. The longest request has exactly 511 cached rows.
All inputs are finite; a program needn't handle non-finite values.
Results may differ from a plain program's by a relative error of at most 0.015.
Values may be sent and summed in bfloat16 or wider, within the bound.
No kernel may reach another device: no remote copies, remote signals or barrier semaphores. Data moves between devices by JAX's collectives and lax.ppermute only.
A program may use at most 64 MiB of HBM per device.

v0:
```python
import math
import jax
import jax.numpy as jnp
from jax import lax
from jax.sharding import PartitionSpec as P

HEAD_DIM = 64
LAYERS = 2
eps_norm = 1e-05
neg_fill = -1e30


def rms_norm(stream):
    as_float = stream.astype(jnp.float32)
    spread = jnp.mean(as_float * as_float, axis=-1, keepdims=True)
    return (as_float * lax.rsqrt(spread + eps_norm)).astype(jnp.bfloat16)


def rotate(heads, positions):
    half_dim = heads.shape[-1] // 2
    inverse = 500000.0 ** (-(2.0 * jnp.arange(half_dim, dtype=jnp.float32)) / heads.shape[-1])
    angles = positions.astype(jnp.float32)[:, None] * inverse[None, :]
    cosine = jnp.cos(angles)[:, None, :]
    sine = jnp.sin(angles)[:, None, :]
    first_half = heads[..., :half_dim]
    second_half = heads[..., half_dim:]
    return jnp.concatenate(
        [first_half * cosine - second_half * sine, second_half * cosine + first_half * sine],
        axis=-1,
    )


def per_device(
    hidden_in,
    lengths,
    positions,
    query_weight,
    key_weight,
    value_weight,
    out_weight,
    gate_weight,
    up_weight,
    down_weight,
    key_cache,
    value_cache,
):
    seq_index = lax.axis_index("seq")
    row_count = query_weight.shape[1]
    row_start = seq_index * row_count
    col_count = out_weight.shape[2]
    col_start = seq_index * col_count
    block_len = key_cache.shape[2]
    kv_width_here = key_cache.shape[3]
    query_width = query_weight.shape[2]
    requests = hidden_in.shape[0]
    group_heads = query_width // HEAD_DIM
    kv_here = kv_width_here // HEAD_DIM
    repeat = group_heads // kv_here
    score_scale = 1.0 / math.sqrt(HEAD_DIM)
    global_slots = seq_index * block_len + jnp.arange(block_len, dtype=jnp.int32)
    new_slot = (global_slots[None, :] == lengths[:, None])[:, :, None]
    live_mask = (global_slots[None, :] <= lengths[:, None])[:, None, None, :]

    def finish(part_terms, stream_now):
        summed = lax.psum(part_terms, "tp")
        own_cols = lax.dynamic_slice_in_dim(stream_now, col_start, col_count, 1).astype(jnp.float32)
        return lax.all_gather((own_cols + summed).astype(jnp.bfloat16), "seq", axis=1, tiled=True)

    stream = hidden_in
    key_layers = []
    value_layers = []
    for layer_idx in range(LAYERS):
        normed = rms_norm(stream)
        own_rows = lax.dynamic_slice_in_dim(normed, row_start, row_count, 1)
        query_part = jnp.dot(own_rows, query_weight[layer_idx], preferred_element_type=jnp.float32)
        key_part = jnp.dot(own_rows, key_weight[layer_idx], preferred_element_type=jnp.float32)
        value_part = jnp.dot(own_rows, value_weight[layer_idx], preferred_element_type=jnp.float32)
        query, key_new, value_new = lax.psum((query_part, key_part, value_part), "seq")
        query = rotate(query.reshape(requests, group_heads, HEAD_DIM), positions).astype(
            jnp.bfloat16
        )
        query = query.reshape(requests, kv_here, repeat, HEAD_DIM)
        key_new = (
            rotate(key_new.reshape(requests, kv_here, HEAD_DIM), positions)
            .astype(jnp.bfloat16)
            .reshape(requests, kv_width_here)
        )
        value_new = value_new.astype(jnp.bfloat16)
        key_rows = jnp.where(new_slot, key_new[:, None, :], key_cache[layer_idx])
        value_rows = jnp.where(new_slot, value_new[:, None, :], value_cache[layer_idx])
        key_heads = key_rows.reshape(requests, block_len, kv_here, HEAD_DIM)
        value_heads = value_rows.reshape(requests, block_len, kv_here, HEAD_DIM)
        scores = (
            jnp.einsum("bkrd,bskd->bkrs", query, key_heads, preferred_element_type=jnp.float32)
            * score_scale
        )
        scores = jnp.where(live_mask, scores, neg_fill)
        row_top = lax.pmax(jnp.max(scores, axis=3), "seq")
        weights = jnp.where(live_mask, jnp.exp(scores - row_top[..., None]), 0.0)
        local_sums = jnp.sum(weights, axis=3)
        local_acc = jnp.einsum(
            "bkrs,bskd->bkrd",
            weights.astype(jnp.bfloat16),
            value_heads,
            preferred_element_type=jnp.float32,
        )
        totals, weighted = lax.psum((local_sums, local_acc), "seq")
        attended = (
            (weighted / totals[..., None]).astype(jnp.bfloat16).reshape(requests, query_width)
        )
        attn_terms = jnp.dot(attended, out_weight[layer_idx], preferred_element_type=jnp.float32)
        mid = finish(attn_terms, stream)
        normed_two = rms_norm(mid)
        rows_two = lax.dynamic_slice_in_dim(normed_two, row_start, row_count, 1)
        gate_part = jnp.dot(rows_two, gate_weight[layer_idx], preferred_element_type=jnp.float32)
        up_part = jnp.dot(rows_two, up_weight[layer_idx], preferred_element_type=jnp.float32)
        gate_sum, up_sum = lax.psum((gate_part, up_part), "seq")
        hidden = (jax.nn.silu(gate_sum) * up_sum).astype(jnp.bfloat16)
        down_terms = jnp.dot(hidden, down_weight[layer_idx], preferred_element_type=jnp.float32)
        stream = finish(down_terms, mid)
        key_layers.append(key_rows)
        value_layers.append(value_rows)
    return (stream, jnp.stack(key_layers), jnp.stack(value_layers))


def solution(mesh):
    return jax.shard_map(
        per_device,
        mesh=mesh,
        in_specs=(
            P(),
            P(),
            P(),
            P(None, "seq", "tp"),
            P(None, "seq", "tp"),
            P(None, "seq", "tp"),
            P(None, "tp", "seq"),
            P(None, "seq", "tp"),
            P(None, "seq", "tp"),
            P(None, "tp", "seq"),
            P(None, None, "seq", "tp"),
            P(None, None, "seq", "tp"),
        ),
        out_specs=(P(), P(None, None, "seq", "tp"), P(None, None, "seq", "tp")),
        check_vma=False,
    )
```

profile of v0, /device:TPU:0, one launch (start us, length us, event | category | flops | bytes accessed | tf_op | source)
XLA Modules:
  0.0 562.6 jit_solution(6855281874656980006)
XLA Ops:
  7.2 0.9 convert_element_type.105
  8.1 1.0 multiply_reduce_fusion.3
  9.1 1.0 fusion.46
  10.2 1.0 fusion.48
  11.3 1.1 fusion.32
  12.5 1.0 slice.86
  13.5 0.2 squeeze.58
  13.7 39.8 %all-reduce.3 = (bf16[16,128]{1,0:T(8,128)(2,1)S(1)}, f32[16,2,64]{2,1,0:T(2,128)S(1)}, f32[16,8,64]{2,1,0:T(8,128)S(1)}) all-reduce(f32[16,128]{1,0:T(8,128)S(1)} %fusion.46, f32[16,2,64]{2,1,0:T(2,128)S(1)} %reshape.206, f32[16,8,64]{2,1,0:T(8,128)S(1)} %reshape.205), channel_id=1, replica_groups=mesh['seq'=8,'tp'=4] {'seq'}, use_global_device_ids=true, to_apply=%region_5.6 | all-reduce | flops 12288 | bytes 94208 | tf_op jit(solution)/shard_map/psum | solution.py:78
  53.6 0.7 broadcast_in_dim.117
  54.3 1.1 squeeze.56
  55.3 0.1 multiply_cosine_fusion
  55.4 0.1 multiply_subtract_fusion.1
  55.5 0.1 subtract_convert_fusion.1
  55.8 1.7 fusion.88
  57.5 33.0 %pmax.14 = f32[16,2,4]{2,1,0:T(2,128)S(1)} all-reduce(f32[16,2,4]{2,1,0:T(2,128)S(1)} %get-tuple-element.38), channel_id=1, replica_groups=mesh['seq'=8,'tp'=4] {'seq'}, use_global_device_ids=true, to_apply=%region_4.5 | all-reduce | flops 128 | bytes 1024 | tf_op jit(solution)/shard_map/pmax | solution.py:98
  90.5 0.2 fusion.56
  90.7 1.0 fusion.21
  91.8 33.8 %all-reduce.2 = (f32[16,2,4,64]{3,2,1,0:T(4,128)S(1)}, f32[16,2,4]{2,1,0:T(2,128)S(1)}) all-reduce(f32[16,2,4,64]{3,2,1,0:T(4,128)S(1)} %fusion.21, f32[16,2,4]{2,1,0:T(2,128)S(1)} %fusion.56), channel_id=1, replica_groups=mesh['seq'=8,'tp'=4] {'seq'}, use_global_device_ids=true, to_apply=%region_6.7 | all-reduce | flops 8320 | bytes 66560 | tf_op jit(solution)/shard_map/psum | solution.py:107
  125.6 0.1 divide_convert_fusion.1
  125.7 0.1 reshape.207
  125.9 0.1 fusion.30
  126.0 10.1 %psum.131 = f32[16,256]{1,0:T(8,128)S(1)} all-reduce(f32[16,256]{1,0:T(8,128)S(1)} %fusion.30), channel_id=1, replica_groups=mesh['seq'=8,'tp'=4] {'tp'}, use_global_device_ids=true, to_apply=%region_9.10 | all-reduce | flops 4096 | bytes 32768 | tf_op jit(solution)/shard_map/psum | solution.py:65
  136.1 0.7 add_convert_fusion.5
  136.8 30.5 %all_gather.12 = bf16[16,2048]{1,0:T(8,128)(2,1)S(1)} all-gather(bf16[16,256]{1,0:T(8,128)(2,1)S(1)} %add_convert_fusion.5), channel_id=1, replica_groups=mesh['seq'=8,'tp'=4] {'seq'}, dimensions={1}, use_global_device_ids=true | all-gather | bytes 73728 | tf_op jit(solution)/shard_map/all_gather | solution.py:67
  167.3 0.1 multiply_reduce_fusion.2
  167.5 1.0 fusion.10
  168.4 2.3 fusion.12
  170.8 0.7 convert_element_type.131
  171.4 69.2 %all-reduce.11.cloned.1.call-done = (f32[16,2048]{1,0:T(8,128)}, f32[16,2048]{1,0:T(8,128)}) async-done(((f32[16,2048]{1,0:T(8,128)}, f32[16,2048]{1,0:T(8,128)}), (f32[16,2048]{1,0:T(8,128)}, f32[16,2048]{1,0:T(8,128)})) %all-reduce.11.cloned.1.call-update) | async-done | bytes 262160 | tf_op jit(solution)/shard_map/psum | solution.py:117
  240.6 1.6 fusion.8
  242.2 10.1 %psum.134 = f32[16,256]{1,0:T(8,128)S(1)} all-reduce(f32[16,256]{1,0:T(8,128)S(1)} %fusion.8), channel_id=1, replica_groups=mesh['seq'=8,'tp'=4] {'tp'}, use_global_device_ids=true, to_apply=%region_13.14 | all-reduce | flops 4096 | bytes 32768 | tf_op jit(solution)/shard_map/psum | solution.py:65
  252.3 30.5 %all_gather.13 = bf16[16,2048]{1,0:T(8,128)(2,1)S(1)} all-gather(bf16[16,256]{1,0:T(8,128)(2,1)S(1)} %add_convert_fusion.4), channel_id=1, replica_groups=mesh['seq'=8,'tp'=4] {'seq'}, dimensions={1}, use_global_device_ids=true | all-gather | bytes 73728 | tf_op jit(solution)/shard_map/all_gather | solution.py:67
  282.9 0.1 multiply_reduce_fusion.1
  283.0 1.0 fusion.42
  284.0 1.0 fusion.44
  285.1 1.1 fusion.28
  286.4 36.4 %all-reduce.1 = (bf16[16,128]{1,0:T(8,128)(2,1)S(1)}, f32[16,2,64]{2,1,0:T(2,128)S(1)}, f32[16,8,64]{2,1,0:T(8,128)S(1)}) all-reduce(f32[16,128]{1,0:T(8,128)S(1)} %fusion.42, f32[16,2,64]{2,1,0:T(2,128)S(1)} %reshape.209, f32[16,8,64]{2,1,0:T(8,128)S(1)} %reshape.208), channel_id=1, replica_groups=mesh['seq'=8,'tp'=4] {'seq'}, use_global_device_ids=true, to_apply=%region_19.20 | all-reduce | flops 12288 | bytes 94208 | tf_op jit(solution)/shard_map/psum | solution.py:78
  322.8 0.1 multiply_subtract_fusion
  322.9 0.1 maximum_convert_fusion.1
  323.0 0.7 convert_element_type.132
  323.7 0.7 broadcast_in_dim.120
  324.4 1.9 broadcast_select_fusion.1
  326.2 1.2 squeeze.67
  327.4 0.2 squeeze.65
  327.7 0.1 subtract_convert_fusion
  327.8 1.2 fusion.89
  329.0 33.0 %pmax.15 = f32[16,2,4]{2,1,0:T(2,128)S(1)} all-reduce(f32[16,2,4]{2,1,0:T(2,128)S(1)} %get-tuple-element.40), channel_id=1, replica_groups=mesh['seq'=8,'tp'=4] {'seq'}, use_global_device_ids=true, to_apply=%region_18.19 | all-reduce | flops 128 | bytes 1024 | tf_op jit(solution)/shard_map/pmax | solution.py:98
  362.0 0.9 fusion.58
  362.9 1.1 fusion.20
  364.0 34.0 %all-reduce = (f32[16,2,4,64]{3,2,1,0:T(4,128)S(1)}, f32[16,2,4]{2,1,0:T(2,128)S(1)}) all-reduce(f32[16,2,4,64]{3,2,1,0:T(4,128)S(1)} %fusion.20, f32[16,2,4]{2,1,0:T(2,128)S(1)} %fusion.58), channel_id=1, replica_groups=mesh['seq'=8,'tp'=4] {'seq'}, use_global_device_ids=true, to_apply=%region_20.21 | all-reduce | flops 8320 | bytes 66560 | tf_op jit(solution)/shard_map/psum | solution.py:107
  398.0 0.1 divide_convert_fusion
  398.1 0.1 reshape.210
  398.2 1.1 fusion.26
  399.3 10.1 %psum.140 = f32[16,256]{1,0:T(8,128)S(1)} all-reduce(f32[16,256]{1,0:T(8,128)S(1)} %fusion.26), channel_id=1, replica_groups=mesh['seq'=8,'tp'=4] {'tp'}, use_global_device_ids=true, to_apply=%region_23.24 | all-reduce | flops 4096 | bytes 32768 | tf_op jit(solution)/shard_map/psum | solution.py:65
  409.4 30.5 %all_gather.14 = bf16[16,2048]{1,0:T(8,128)(2,1)S(1)} all-gather(bf16[16,256]{1,0:T(8,128)(2,1)S(1)} %add_convert_fusion.3), channel_id=1, replica_groups=mesh['seq'=8,'tp'=4] {'seq'}, dimensions={1}, use_global_device_ids=true | all-gather | bytes 73728 | tf_op jit(solution)/shard_map/all_gather | solution.py:67
  439.9 0.1 multiply_reduce_fusion
  440.0 0.9 fusion.4
  441.0 2.3 fusion.6
  443.4 1.1 pad_maximum_fusion
  444.4 68.8 %all-reduce.9.cloned.1.call-done = (f32[16,2048]{1,0:T(8,128)}, f32[16,2048]{1,0:T(8,128)}) async-done(((f32[16,2048]{1,0:T(8,128)}, f32[16,2048]{1,0:T(8,128)}), (f32[16,2048]{1,0:T(8,128)}, f32[16,2048]{1,0:T(8,128)})) %all-reduce.9.cloned.1.call-update) | async-done | bytes 262160 | tf_op jit(solution)/shard_map/psum | solution.py:117
  513.3 1.2 fusion.2
  514.5 10.1 %psum.143 = f32[16,256]{1,0:T(8,128)S(1)} all-reduce(f32[16,256]{1,0:T(8,128)S(1)} %fusion.2), channel_id=1, replica_groups=mesh['seq'=8,'tp'=4] {'tp'}, use_global_device_ids=true, to_apply=%region_27.28 | all-reduce | flops 4096 | bytes 32768 | tf_op jit(solution)/shard_map/psum | solution.py:65
  524.6 30.5 %all_gather.15 = bf16[16,2048]{1,0:T(8,128)(2,1)S(1)} all-gather(bf16[16,256]{1,0:T(8,128)(2,1)S(1)} %add_convert_fusion.2), channel_id=1, replica_groups=mesh['seq'=8,'tp'=4] {'seq'}, dimensions={1}, use_global_device_ids=true | all-gather | bytes 73728 | tf_op jit(solution)/shard_map/all_gather | solution.py:67
  555.1 0.6 copy.36
  (57 shorter events, 0.8 us)
Async XLA Ops:
  7.2 47.1 %slice-start = ((bf16[2,16,64,128]{3,2,1,0:T(8,128)(2,1)}), bf16[1,16,64,128]{3,2,1,0:T(8,128)(2,1)S(1)}, s32[]{:S(2)}) async-start(bf16[2,16,64,128]{3,2,1,0:T(8,128)(2,1)} %param.22), calls=%async_computation.2 | async-start | bytes 524288 | tf_op jit(solution)/shard_map/slice | solution.py:89
  7.2 48.1 %copy-start.15 = (s32[16]{0:T(128)S(1)}, s32[16]{0:T(128)}, u32[]{:S(2)}) copy-start(s32[16]{0:T(128)} %param.14) | copy-start | bytes 196
  7.2 48.5 %copy-start.13 = (s32[16]{0:T(128)S(1)}, s32[16]{0:T(128)}, u32[]{:S(2)}) copy-start(s32[16]{0:T(128)} %param.13) | copy-start | bytes 196
  7.2 233.4 %all-reduce.11.cloned.1.call-start = ((), (), s32[]{:S(2)}) async-start(), calls=%async_computation.1 | async-start | bytes 524288 | tf_op jit(solution)/shard_map/psum | solution.py:117
  53.6 0.7 copy-start.10
  54.3 71.6 %copy-start.7 = (bf16[2,512,256]{2,1,0:T(8,128)(2,1)S(1)}, bf16[2,512,256]{2,1,0:T(8,128)(2,1)}, u32[]{:S(2)}) copy-start(bf16[2,512,256]{2,1,0:T(8,128)(2,1)} %param.18) | copy-start | bytes 1572868
  55.5 111.9 %copy-start = (bf16[2,256,2048]{2,1,0:T(8,128)(2,1)S(1)}, bf16[2,256,2048]{2,1,0:T(8,128)(2,1)}, u32[]{:S(2)}) copy-start(bf16[2,256,2048]{2,1,0:T(8,128)(2,1)} %param.20) | copy-start | bytes 6291460
  55.7 112.7 %copy-start.9 = (pred[16,64]{1,0:T(8,128)(4,1)}, pred[16,64]{1,0:T(8,128)(4,1)S(1)}, u32[]{:S(2)}) copy-start(pred[16,64]{1,0:T(8,128)(4,1)S(1)} %get-tuple-element.34) | copy-start | bytes 3076
  55.7 112.7 %copy-start.12 = (pred[16,64]{1,0:T(8,128)(4,1)}, pred[16,64]{1,0:T(8,128)(4,1)S(1)}, u32[]{:S(2)}) copy-start(pred[16,64]{1,0:T(8,128)(4,1)S(1)} %get-tuple-element.35) | copy-start | bytes 3076
  168.4 155.9 %copy-start.1 = (bf16[2,16,64,128]{3,2,1,0:T(8,128)(2,1)S(1)}, bf16[2,16,64,128]{3,2,1,0:T(8,128)(2,1)}, u32[]{:S(2)}) copy-start(bf16[2,16,64,128]{3,2,1,0:T(8,128)(2,1)} %param.23) | copy-start | bytes 1572868
  168.4 155.9 %copy-start.2 = (bf16[2,16,64,128]{3,2,1,0:T(8,128)(2,1)S(1)}, bf16[2,16,64,128]{3,2,1,0:T(8,128)(2,1)}, u32[]{:S(2)}) copy-start(bf16[2,16,64,128]{3,2,1,0:T(8,128)(2,1)} %param.22) | copy-start | bytes 1572868
  170.7 342.6 %all-reduce.9.cloned.1.call-start = ((), (), s32[]{:S(2)}) async-start(), calls=%async_computation | async-start | bytes 524288 | tf_op jit(solution)/shard_map/psum | solution.py:117
  322.8 0.9 copy-start.11
  323.0 0.7 copy-start.8
  364.0 79.4 %copy-start.3 = (bf16[1,16,64,128]{3,2,1,0:T(8,128)(2,1)S(1)}, bf16[1,16,64,128]{3,2,1,0:T(8,128)(2,1)}, u32[]{:S(2)}) copy-start(bf16[1,16,64,128]{3,2,1,0:T(8,128)(2,1)} %get-tuple-element.17) | copy-start | bytes 786436
  364.0 79.4 %copy-start.4 = (bf16[1,16,64,128]{3,2,1,0:T(8,128)(2,1)S(1)}, bf16[1,16,64,128]{3,2,1,0:T(8,128)(2,1)}, u32[]{:S(2)}) copy-start(bf16[1,16,64,128]{3,2,1,0:T(8,128)(2,1)} %get-tuple-element.18) | copy-start | bytes 786436
  364.0 79.4 %copy-start.5 = (bf16[1,16,64,128]{3,2,1,0:T(8,128)(2,1)S(1)}, bf16[1,16,64,128]{3,2,1,0:T(8,128)(2,1)}, u32[]{:S(2)}) copy-start(bf16[1,16,64,128]{3,2,1,0:T(8,128)(2,1)} %get-tuple-element.32) | copy-start | bytes 786436
  364.0 79.4 %copy-start.6 = (bf16[1,16,64,128]{3,2,1,0:T(8,128)(2,1)S(1)}, bf16[1,16,64,128]{3,2,1,0:T(8,128)(2,1)}, u32[]{:S(2)}) copy-start(bf16[1,16,64,128]{3,2,1,0:T(8,128)(2,1)} %get-tuple-element.33) | copy-start | bytes 786436
  441.0 72.3 %copy-start.14 = (bf16[2,2048,256]{2,1,0:T(8,128)(2,1)S(1)}, bf16[2,2048,256]{2,1,0:T(8,128)(2,1)}, u32[]{:S(2)}) copy-start(bf16[2,2048,256]{2,1,0:T(8,128)(2,1)} %param.21) | copy-start | bytes 6291460
Sparse Core Ops, SparseCore 0:
  170.8 69.7 all-reduce.10
  443.5 69.7 all-reduce.8
where the time goes:
time: 564 us; the launch traced here: 563 us
  blocking collectives  372 us (66%)
  waiting for transfers between devices  138 us (24%)
  matrix products  22 us (4%)
  between operations  14.4 us (3%)
  other arithmetic  8.02 us (1%)
  local copies, waits for them, and re-layouts  7.62 us (1%)
    psum x2, waiting for transfers between devices, per_device(): gate_sum, up_sum = lax.psum((gate_part, up_part), 'seq')  138 us
    all_gather x4, blocking collectives, finish(): lax.all_gather((own_cols + summed).astype(jnp.bfloat16), 'seq', axis=1, t...  122 us
    psum x2, blocking collectives, per_device(): lax.psum((query_part, key_part, value_part), 'seq')  76.3 us
    psum x2, blocking collectives, per_device(): totals, weighted = lax.psum((local_sums, local_acc), 'seq')  67.8 us
    pmax x2, blocking collectives, per_device(): row_top = lax.pmax(jnp.max(scores, axis=3), 'seq')  66 us
    psum x4, blocking collectives, finish(): summed = lax.psum(part_terms, 'tp')  40.5 us
  transfers between devices with their start and end apart: 2, of which 2 were waited for; matrix products, arithmetic and copies ran while one was open for 0% of the time, Pallas kernels for 0%

commit v1 on v0

--- a/solution.py
+++ b/solution.py
@@ -8,6 +8,24 @@
 LAYERS = 2
 eps_norm = 1e-05
 neg_fill = -1e30
+
+
+def gather_around(array, axis, dim):
+    ways, here, step = (lax.axis_size(axis), lax.axis_index(axis), array.shape[dim])
+    shape = [n * ways if d == dim else n for d, n in enumerate(array.shape)]
+    full = lax.dynamic_update_slice_in_dim(
+        jnp.zeros(shape, array.dtype), array, here * step, axis=dim
+    )
+    going_up = going_down = array
+    for far in range(1, ways // 2 + 1):
+        going_up = lax.ppermute(going_up, axis, [(d, (d + 1) % ways) for d in range(ways)])
+        full = lax.dynamic_update_slice_in_dim(full, going_up, (here - far) % ways * step, axis=dim)
+        if 2 * far < ways:
+            going_down = lax.ppermute(going_down, axis, [(d, (d - 1) % ways) for d in range(ways)])
+            full = lax.dynamic_update_slice_in_dim(
+                full, going_down, (here + far) % ways * step, axis=dim
+            )
+    return full
 
 
 def rms_norm(stream):
@@ -64,7 +82,7 @@
     def finish(part_terms, stream_now):
         summed = lax.psum(part_terms, "tp")
         own_cols = lax.dynamic_slice_in_dim(stream_now, col_start, col_count, 1).astype(jnp.float32)
-        return lax.all_gather((own_cols + summed).astype(jnp.bfloat16), "seq", axis=1, tiled=True)
+        return gather_around((own_cols + summed).astype(jnp.bfloat16), "seq", 1)
 
     stream = hidden_in
     key_layers = []

time: 564 us -> 540 us (0.957)
  blocking collectives: 372 us -> 250 us
  starting transfers between devices: 0.08 us -> 57.9 us
  waiting for transfers between devices: 138 us -> 179 us
    all_gather x4 -> x0, blocking collectives: 122 us -> none  [finish(): lax.all_gather((own_cols + summed).astype(jnp.bfloat16), 'seq', axis=1, t...]
    ppermute x0 -> x28, starting transfers between devices: none -> 57.9 us  [the longest x12 56.1 us: gather_around(): lax.ppermute(going_down, axis, [(d, (d - 1) % ways) for d in range(ways)])]
    ppermute x0 -> x28, waiting for transfers between devices: none -> 42 us  [the longest x16 38.3 us: gather_around(): lax.ppermute(going_up, axis, [(d, (d + 1) % ways) for d in range(ways)])]
  transfers between devices with their start and end apart: 2 -> 30, of which waited for: 2 -> 24; matrix products, arithmetic and copies ran while one was open for 0% -> 0% of each run, Pallas kernels for 0% -> 0%
where the time goes in v1:
time: 540 us; the launch traced here: 539 us
  blocking collectives  250 us (46%)
  waiting for transfers between devices  179 us (33%)
  starting transfers between devices  57.9 us (11%)
  matrix products  21.6 us (4%)
  between operations  14.5 us (3%)
  local copies, waits for them, and re-layouts  8.52 us (2%)
  other arithmetic  8.07 us (1%)
    psum x2, waiting for transfers between devices, per_device(): gate_sum, up_sum = lax.psum((gate_part, up_part), 'seq')  137 us
    psum x2, blocking collectives, per_device(): lax.psum((query_part, key_part, value_part), 'seq')  73.7 us
    pmax x2, blocking collectives, per_device(): row_top = lax.pmax(jnp.max(scores, axis=3), 'seq')  67.9 us
    psum x2, blocking collectives, per_device(): totals, weighted = lax.psum((local_sums, local_acc), 'seq')  67.7 us
    ppermute x12, starting transfers between devices, gather_around(): lax.ppermute(going_down, axis, [(d, (d - 1) % ways) for d in range(ways)])  56.1 us
    psum x4, blocking collectives, finish(): summed = lax.psum(part_terms, 'tp')  40.5 us
    ppermute x16, waiting for transfers between devices, gather_around(): lax.ppermute(going_up, axis, [(d, (d + 1) % ways) for d in range(ways)])  38.3 us
  transfers between devices with their start and end apart: 30, of which 24 were waited for; matrix products, arithmetic and copies ran while one was open for 0% of the time, Pallas kernels for 0%

profile of v1, /device:TPU:0, one launch (start us, length us, event | category | flops | bytes accessed | tf_op | source)
XLA Modules:
  0.0 538.9 jit_solution(11210561653272061348)
XLA Ops:
  7.2 0.9 convert_element_type.105
  8.1 1.0 multiply_reduce_fusion.3
  9.1 1.0 fusion.46
  10.2 1.0 fusion.48
  11.3 1.1 fusion.32
  12.5 1.0 slice.86
  13.7 39.8 %all-reduce.3 = (bf16[16,128]{1,0:T(8,128)(2,1)S(1)}, f32[16,2,64]{2,1,0:T(2,128)S(1)}, f32[16,8,64]{2,1,0:T(8,128)S(1)}) all-reduce(f32[16,128]{1,0:T(8,128)S(1)} %fusion.46, f32[16,2,64]{2,1,0:T(2,128)S(1)} %reshape.206, f32[16,8,64]{2,1,0:T(8,128)S(1)} %reshape.205), channel_id=1, replica_groups=mesh['seq'=8,'tp'=4] {'seq'}, use_global_device_ids=true, to_apply=%region_5.6 | all-reduce | flops 12288 | bytes 94208 | tf_op jit(solution)/shard_map/psum | solution.py:96
  54.3 1.1 squeeze.56
  55.8 1.7 fusion.88
  57.5 33.0 %pmax.14 = f32[16,2,4]{2,1,0:T(2,128)S(1)} all-reduce(f32[16,2,4]{2,1,0:T(2,128)S(1)} %get-tuple-element.46), channel_id=1, replica_groups=mesh['seq'=8,'tp'=4] {'seq'}, use_global_device_ids=true, to_apply=%region_4.5 | all-reduce | flops 128 | bytes 1024 | tf_op jit(solution)/shard_map/pmax | solution.py:116
  90.7 1.0 fusion.21
  91.8 33.8 %all-reduce.2 = (f32[16,2,4,64]{3,2,1,0:T(4,128)S(1)}, f32[16,2,4]{2,1,0:T(2,128)S(1)}) all-reduce(f32[16,2,4,64]{3,2,1,0:T(4,128)S(1)} %fusion.21, f32[16,2,4]{2,1,0:T(2,128)S(1)} %fusion.56), channel_id=1, replica_groups=mesh['seq'=8,'tp'=4] {'seq'}, use_global_device_ids=true, to_apply=%region_6.7 | all-reduce | flops 8320 | bytes 66560 | tf_op jit(solution)/shard_map/psum | solution.py:125
  126.0 10.1 %psum.131 = f32[16,256]{1,0:T(8,128)S(1)} all-reduce(f32[16,256]{1,0:T(8,128)S(1)} %fusion.30), channel_id=1, replica_groups=mesh['seq'=8,'tp'=4] {'tp'}, use_global_device_ids=true, to_apply=%region_9.10 | all-reduce | flops 4096 | bytes 32768 | tf_op jit(solution)/shard_map/psum | solution.py:83
  136.8 4.7 collective-permute-start.1
  141.6 1.6 collective-permute-done
  143.2 4.7 collective-permute-start.3
  147.9 1.6 collective-permute-done.2
  149.5 4.7 collective-permute-start.5
  154.3 1.6 collective-permute-done.4
  155.9 6.3 %collective-permute-done.6 = bf16[16,256]{1,0:T(8,128)(2,1)S(1)} collective-permute-done((bf16[16,256]{1,0:T(8,128)(2,1)S(1)}, bf16[16,256]{1,0:T(8,128)(2,1)S(1)}, u32[]{:S(2)}, u32[]{:S(2)}) %collective-permute-start.6) | collective-permute-done | bytes 8224 | tf_op jit(solution)/shard_map/ppermute | solution.py:21
  162.4 1.0 fusion.10
  163.4 2.3 fusion.12
  165.7 68.3 %all-reduce.11.cloned.1.call-done = (f32[16,2048]{1,0:T(8,128)}, f32[16,2048]{1,0:T(8,128)}) async-done(((f32[16,2048]{1,0:T(8,128)}, f32[16,2048]{1,0:T(8,128)}), (f32[16,2048]{1,0:T(8,128)}, f32[16,2048]{1,0:T(8,128)})) %all-reduce.11.cloned.1.call-update) | async-done | bytes 262160 | tf_op jit(solution)/shard_map/psum | solution.py:135
  234.0 1.6 fusion.8
  235.6 10.1 %psum.134 = f32[16,256]{1,0:T(8,128)S(1)} all-reduce(f32[16,256]{1,0:T(8,128)S(1)} %fusion.8), channel_id=1, replica_groups=mesh['seq'=8,'tp'=4] {'tp'}, use_global_device_ids=true, to_apply=%region_13.14 | all-reduce | flops 4096 | bytes 32768 | tf_op jit(solution)/shard_map/psum | solution.py:83
  245.7 0.8 collective-permute-start.7
  247.2 3.9 collective-permute-start.8
  251.2 0.9 collective-permute-done.7
  252.6 5.0 collective-permute-start.10
  257.5 0.9 collective-permute-done.9
  258.9 5.0 collective-permute-start.12
  263.9 0.9 collective-permute-done.11
  265.3 5.9 %collective-permute-done.13 = bf16[16,256]{1,0:T(8,128)(2,1)S(1)} collective-permute-done((bf16[16,256]{1,0:T(8,128)(2,1)S(1)}, bf16[16,256]{1,0:T(8,128)(2,1)S(1)}, u32[]{:S(2)}, u32[]{:S(2)}) %collective-permute-start.13) | collective-permute-done | bytes 8224 | tf_op jit(solution)/shard_map/ppermute | solution.py:21
  271.3 1.0 fusion.42
  272.4 1.0 fusion.44
  273.4 1.1 fusion.28
  274.7 33.9 %all-reduce.1 = (bf16[16,128]{1,0:T(8,128)(2,1)S(1)}, f32[16,2,64]{2,1,0:T(2,128)S(1)}, f32[16,8,64]{2,1,0:T(8,128)S(1)}) all-reduce(f32[16,128]{1,0:T(8,128)S(1)} %fusion.42, f32[16,2,64]{2,1,0:T(2,128)S(1)} %reshape.209, f32[16,8,64]{2,1,0:T(8,128)S(1)} %reshape.208), channel_id=1, replica_groups=mesh['seq'=8,'tp'=4] {'seq'}, use_global_device_ids=true, to_apply=%region_19.20 | all-reduce | flops 12288 | bytes 94208 | tf_op jit(solution)/shard_map/psum | solution.py:96
  310.1 1.9 broadcast_select_fusion.1
  312.1 1.2 squeeze.67
  313.3 1.1 squeeze.65
  314.4 1.6 fusion.89
  316.0 34.9 %pmax.15 = f32[16,2,4]{2,1,0:T(2,128)S(1)} all-reduce(f32[16,2,4]{2,1,0:T(2,128)S(1)} %get-tuple-element.48), channel_id=1, replica_groups=mesh['seq'=8,'tp'=4] {'seq'}, use_global_device_ids=true, to_apply=%region_18.19 | all-reduce | flops 128 | bytes 1024 | tf_op jit(solution)/shard_map/pmax | solution.py:116
  350.9 0.9 fusion.58
  351.8 1.1 fusion.20
  352.9 33.8 %all-reduce = (f32[16,2,4,64]{3,2,1,0:T(4,128)S(1)}, f32[16,2,4]{2,1,0:T(2,128)S(1)}) all-reduce(f32[16,2,4,64]{3,2,1,0:T(4,128)S(1)} %fusion.20, f32[16,2,4]{2,1,0:T(2,128)S(1)} %fusion.58), channel_id=1, replica_groups=mesh['seq'=8,'tp'=4] {'seq'}, use_global_device_ids=true, to_apply=%region_20.21 | all-reduce | flops 8320 | bytes 66560 | tf_op jit(solution)/shard_map/psum | solution.py:125
  387.1 10.1 %psum.140 = f32[16,256]{1,0:T(8,128)S(1)} all-reduce(f32[16,256]{1,0:T(8,128)S(1)} %fusion.26), channel_id=1, replica_groups=mesh['seq'=8,'tp'=4] {'tp'}, use_global_device_ids=true, to_apply=%region_23.24 | all-reduce | flops 4096 | bytes 32768 | tf_op jit(solution)/shard_map/psum | solution.py:83
  397.3 4.7 collective-permute-start.15
  402.0 1.6 collective-permute-done.14
  403.6 4.7 collective-permute-start.17
  408.4 1.6 collective-permute-done.16
  410.0 4.7 collective-permute-start.19
  414.7 1.6 collective-permute-done.18
  416.4 6.3 %collective-permute-done.20 = bf16[16,256]{1,0:T(8,128)(2,1)S(1)} collective-permute-done((bf16[16,256]{1,0:T(8,128)(2,1)S(1)}, bf16[16,256]{1,0:T(8,128)(2,1)S(1)}, u32[]{:S(2)}, u32[]{:S(2)}) %collective-permute-start.20) | collective-permute-done | bytes 8224 | tf_op jit(solution)/shard_map/ppermute | solution.py:21
  422.9 1.0 fusion.4
  423.8 2.2 fusion.6
  426.0 68.3 %all-reduce.9.cloned.1.call-done = (f32[16,2048]{1,0:T(8,128)}, f32[16,2048]{1,0:T(8,128)}) async-done(((f32[16,2048]{1,0:T(8,128)}, f32[16,2048]{1,0:T(8,128)}), (f32[16,2048]{1,0:T(8,128)}, f32[16,2048]{1,0:T(8,128)})) %all-reduce.9.cloned.1.call-update) | async-done | bytes 262160 | tf_op jit(solution)/shard_map/psum | solution.py:135
  494.3 1.6 fusion.2
  495.9 10.1 %psum.143 = f32[16,256]{1,0:T(8,128)S(1)} all-reduce(f32[16,256]{1,0:T(8,128)S(1)} %fusion.2), channel_id=1, replica_groups=mesh['seq'=8,'tp'=4] {'tp'}, use_global_device_ids=true, to_apply=%region_27.28 | all-reduce | flops 4096 | bytes 32768 | tf_op jit(solution)/shard_map/psum | solution.py:83
  506.0 0.8 collective-permute-start.21
  506.9 1.1 pad_maximum_fusion
  507.9 3.9 collective-permute-start.22
  513.2 5.0 collective-permute-start.24
  519.6 5.0 collective-permute-start.26
  525.9 5.5 %collective-permute-done.27 = bf16[16,256]{1,0:T(8,128)(2,1)S(1)} collective-permute-done((bf16[16,256]{1,0:T(8,128)(2,1)S(1)}, bf16[16,256]{1,0:T(8,128)(2,1)S(1)}, u32[]{:S(2)}, u32[]{:S(2)}) %collective-permute-start.27) | collective-permute-done | bytes 8224 | tf_op jit(solution)/shard_map/ppermute | solution.py:21
  (142 shorter events, 12.5 us)
Async XLA Ops:
  7.2 47.1 %slice-start = ((bf16[2,16,64,128]{3,2,1,0:T(8,128)(2,1)}), bf16[1,16,64,128]{3,2,1,0:T(8,128)(2,1)S(1)}, s32[]{:S(2)}) async-start(bf16[2,16,64,128]{3,2,1,0:T(8,128)(2,1)} %param.22), calls=%async_computation.2 | async-start | bytes 524288 | tf_op jit(solution)/shard_map/slice | solution.py:107
  7.2 48.1 %copy-start.16 = (s32[16]{0:T(128)S(1)}, s32[16]{0:T(128)}, u32[]{:S(2)}) copy-start(s32[16]{0:T(128)} %param.14) | copy-start | bytes 196
  7.2 48.4 %copy-start.15 = (s32[16]{0:T(128)S(1)}, s32[16]{0:T(128)}, u32[]{:S(2)}) copy-start(s32[16]{0:T(128)} %param.13) | copy-start | bytes 196
  7.2 226.8 %all-reduce.11.cloned.1.call-start = ((), (), s32[]{:S(2)}) async-start(), calls=%async_computation.1 | async-start | bytes 524288 | tf_op jit(solution)/shard_map/psum | solution.py:135
  53.6 0.7 copy-start.12
  54.2 71.6 %copy-start.7 = (bf16[2,512,256]{2,1,0:T(8,128)(2,1)S(1)}, bf16[2,512,256]{2,1,0:T(8,128)(2,1)}, u32[]{:S(2)}) copy-start(bf16[2,512,256]{2,1,0:T(8,128)(2,1)} %param.18) | copy-start | bytes 1572868
  55.7 106.5 %copy-start.11 = (pred[16,64]{1,0:T(8,128)(4,1)}, pred[16,64]{1,0:T(8,128)(4,1)S(1)}, u32[]{:S(2)}) copy-start(pred[16,64]{1,0:T(8,128)(4,1)S(1)} %get-tuple-element.42) | copy-start | bytes 3076
  55.7 106.5 %copy-start.14 = (pred[16,64]{1,0:T(8,128)(4,1)}, pred[16,64]{1,0:T(8,128)(4,1)S(1)}, u32[]{:S(2)}) copy-start(pred[16,64]{1,0:T(8,128)(4,1)S(1)} %get-tuple-element.43) | copy-start | bytes 3076
  55.8 106.6 %copy-start = (bf16[2,256,2048]{2,1,0:T(8,128)(2,1)S(1)}, bf16[2,256,2048]{2,1,0:T(8,128)(2,1)}, u32[]{:S(2)}) copy-start(bf16[2,256,2048]{2,1,0:T(8,128)(2,1)} %param.20) | copy-start | bytes 6291460
  136.8 6.3 %collective-permute-start = (bf16[16,256]{1,0:T(8,128)(2,1)S(1)}, bf16[16,256]{1,0:T(8,128)(2,1)S(1)}, u32[]{:S(2)}, u32[]{:S(2)}) collective-permute-start(bf16[16,256]{1,0:T(8,128)(2,1)S(1)} %get-tuple-element.24), channel_id=1, source_target_pairs={{0,4},{4,8},{8,12},{12,16},{16,20},{20,24},{24,28},{28,0},{1,5},{5... | collective-permute-start | bytes 24584 | tf_op jit(solution)/shard_map/ppermute | solution.py:21
  136.8 6.4 %collective-permute-start.1 = (bf16[16,256]{1,0:T(8,128)(2,1)S(1)}, bf16[16,256]{1,0:T(8,128)(2,1)S(1)}, u32[]{:S(2)}, u32[]{:S(2)}) collective-permute-start(bf16[16,256]{1,0:T(8,128)(2,1)S(1)} %get-tuple-element.24), channel_id=1, source_target_pairs={{0,28},{4,0},{8,4},{12,8},{16,12},{20,16},{24,20},{28,24},{1,29},{... | collective-permute-start | bytes 24584 | tf_op jit(solution)/shard_map/ppermute | solution.py:24
  143.2 6.3 %collective-permute-start.2 = (bf16[16,256]{1,0:T(8,128)(2,1)S(1)}, bf16[16,256]{1,0:T(8,128)(2,1)S(1)}, u32[]{:S(2)}, u32[]{:S(2)}) collective-permute-start(bf16[16,256]{1,0:T(8,128)(2,1)S(1)} %collective-permute-done), channel_id=1, source_target_pairs={{0,4},{4,8},{8,12},{12,16},{16,20},{20,24},{24,28},{28,0},{1,5},{5... | collective-permute-start | bytes 24584 | tf_op jit(solution)/shard_map/ppermute | solution.py:21
  143.2 6.3 %collective-permute-start.3 = (bf16[16,256]{1,0:T(8,128)(2,1)S(1)}, bf16[16,256]{1,0:T(8,128)(2,1)S(1)}, u32[]{:S(2)}, u32[]{:S(2)}) collective-permute-start(bf16[16,256]{1,0:T(8,128)(2,1)S(1)} %collective-permute-done.1), channel_id=1, source_target_pairs={{0,28},{4,0},{8,4},{12,8},{16,12},{20,16},{24,20},{28,24},{1,29},{... | collective-permute-start | bytes 24584 | tf_op jit(solution)/shard_map/ppermute | solution.py:24
  149.5 6.3 %collective-permute-start.4 = (bf16[16,256]{1,0:T(8,128)(2,1)S(1)}, bf16[16,256]{1,0:T(8,128)(2,1)S(1)}, u32[]{:S(2)}, u32[]{:S(2)}) collective-permute-start(bf16[16,256]{1,0:T(8,128)(2,1)S(1)} %collective-permute-done.2), channel_id=1, source_target_pairs={{0,4},{4,8},{8,12},{12,16},{16,20},{20,24},{24,28},{28,0},{1,5},{5... | collective-permute-start | bytes 24584 | tf_op jit(solution)/shard_map/ppermute | solution.py:21
  149.5 6.3 %collective-permute-start.5 = (bf16[16,256]{1,0:T(8,128)(2,1)S(1)}, bf16[16,256]{1,0:T(8,128)(2,1)S(1)}, u32[]{:S(2)}, u32[]{:S(2)}) collective-permute-start(bf16[16,256]{1,0:T(8,128)(2,1)S(1)} %collective-permute-done.3), channel_id=1, source_target_pairs={{0,28},{4,0},{8,4},{12,8},{16,12},{20,16},{24,20},{28,24},{1,29},{... | collective-permute-start | bytes 24584 | tf_op jit(solution)/shard_map/ppermute | solution.py:24
  155.9 6.3 %collective-permute-start.6 = (bf16[16,256]{1,0:T(8,128)(2,1)S(1)}, bf16[16,256]{1,0:T(8,128)(2,1)S(1)}, u32[]{:S(2)}, u32[]{:S(2)}) collective-permute-start(bf16[16,256]{1,0:T(8,128)(2,1)S(1)} %collective-permute-done.4), channel_id=1, source_target_pairs={{0,4},{4,8},{8,12},{12,16},{16,20},{20,24},{24,28},{28,0},{1,5},{5... | collective-permute-start | bytes 24584 | tf_op jit(solution)/shard_map/ppermute | solution.py:21
  163.4 146.8 %copy-start.1 = (bf16[2,16,64,128]{3,2,1,0:T(8,128)(2,1)S(1)}, bf16[2,16,64,128]{3,2,1,0:T(8,128)(2,1)}, u32[]{:S(2)}) copy-start(bf16[2,16,64,128]{3,2,1,0:T(8,128)(2,1)} %param.23) | copy-start | bytes 1572868
  163.4 146.8 %copy-start.2 = (bf16[2,16,64,128]{3,2,1,0:T(8,128)(2,1)S(1)}, bf16[2,16,64,128]{3,2,1,0:T(8,128)(2,1)}, u32[]{:S(2)}) copy-start(bf16[2,16,64,128]{3,2,1,0:T(8,128)(2,1)} %param.22) | copy-start | bytes 1572868
  165.6 328.6 %all-reduce.9.cloned.1.call-start = ((), (), s32[]{:S(2)}) async-start(), calls=%async_computation | async-start | bytes 524288 | tf_op jit(solution)/shard_map/psum | solution.py:135
  245.7 6.4 %collective-permute-start.7 = (bf16[16,256]{1,0:T(8,128)(2,1)S(1)}, bf16[16,256]{1,0:T(8,128)(2,1)S(1)}, u32[]{:S(2)}, u32[]{:S(2)}) collective-permute-start(bf16[16,256]{1,0:T(8,128)(2,1)S(1)} %get-tuple-element.22), channel_id=1, source_target_pairs={{0,4},{4,8},{8,12},{12,16},{16,20},{20,24},{24,28},{28,0},{1,5},{5... | collective-permute-start | bytes 24584 | tf_op jit(solution)/shard_map/ppermute | solution.py:21
  247.2 5.3 collective-permute-start.8
  252.1 6.3 %collective-permute-start.9 = (bf16[16,256]{1,0:T(8,128)(2,1)S(1)}, bf16[16,256]{1,0:T(8,128)(2,1)S(1)}, u32[]{:S(2)}, u32[]{:S(2)}) collective-permute-start(bf16[16,256]{1,0:T(8,128)(2,1)S(1)} %collective-permute-done.7), channel_id=1, source_target_pairs={{0,4},{4,8},{8,12},{12,16},{16,20},{20,24},{24,28},{28,0},{1,5},{5... | collective-permute-start | bytes 24584 | tf_op jit(solution)/shard_map/ppermute | solution.py:21
  252.6 6.3 %collective-permute-start.10 = (bf16[16,256]{1,0:T(8,128)(2,1)S(1)}, bf16[16,256]{1,0:T(8,128)(2,1)S(1)}, u32[]{:S(2)}, u32[]{:S(2)}) collective-permute-start(bf16[16,256]{1,0:T(8,128)(2,1)S(1)} %collective-permute-done.8), channel_id=1, source_target_pairs={{0,28},{4,0},{8,4},{12,8},{16,12},{20,16},{24,20},{28,24},{1,29},{... | collective-permute-start | bytes 24584 | tf_op jit(solution)/shard_map/ppermute | solution.py:24
  258.5 6.3 %collective-permute-start.11 = (bf16[16,256]{1,0:T(8,128)(2,1)S(1)}, bf16[16,256]{1,0:T(8,128)(2,1)S(1)}, u32[]{:S(2)}, u32[]{:S(2)}) collective-permute-start(bf16[16,256]{1,0:T(8,128)(2,1)S(1)} %collective-permute-done.9), channel_id=1, source_target_pairs={{0,4},{4,8},{8,12},{12,16},{16,20},{20,24},{24,28},{28,0},{1,5},{5... | collective-permute-start | bytes 24584 | tf_op jit(solution)/shard_map/ppermute | solution.py:21
  258.9 6.3 %collective-permute-start.12 = (bf16[16,256]{1,0:T(8,128)(2,1)S(1)}, bf16[16,256]{1,0:T(8,128)(2,1)S(1)}, u32[]{:S(2)}, u32[]{:S(2)}) collective-permute-start(bf16[16,256]{1,0:T(8,128)(2,1)S(1)} %collective-permute-done.10), channel_id=1, source_target_pairs={{0,28},{4,0},{8,4},{12,8},{16,12},{20,16},{24,20},{28,24},{1,29},{... | collective-permute-start | bytes 24584 | tf_op jit(solution)/shard_map/ppermute | solution.py:24
  264.8 6.3 %collective-permute-start.13 = (bf16[16,256]{1,0:T(8,128)(2,1)S(1)}, bf16[16,256]{1,0:T(8,128)(2,1)S(1)}, u32[]{:S(2)}, u32[]{:S(2)}) collective-permute-start(bf16[16,256]{1,0:T(8,128)(2,1)S(1)} %collective-permute-done.11), channel_id=1, source_target_pairs={{0,4},{4,8},{8,12},{12,16},{16,20},{20,24},{24,28},{28,0},{1,5},{5... | collective-permute-start | bytes 24584 | tf_op jit(solution)/shard_map/ppermute | solution.py:21
  308.6 0.9 copy-start.13
  308.8 0.7 copy-start.10
  313.3 73.7 %copy-start.8 = (bf16[2,512,256]{2,1,0:T(8,128)(2,1)S(1)}, bf16[2,512,256]{2,1,0:T(8,128)(2,1)}, u32[]{:S(2)}) copy-start(bf16[2,512,256]{2,1,0:T(8,128)(2,1)} %param.18) | copy-start | bytes 1572868
  397.2 6.4 %collective-permute-start.14 = (bf16[16,256]{1,0:T(8,128)(2,1)S(1)}, bf16[16,256]{1,0:T(8,128)(2,1)S(1)}, u32[]{:S(2)}, u32[]{:S(2)}) collective-permute-start(bf16[16,256]{1,0:T(8,128)(2,1)S(1)} %get-tuple-element.20), channel_id=1, source_target_pairs={{0,4},{4,8},{8,12},{12,16},{16,20},{20,24},{24,28},{28,0},{1,5},{5... | collective-permute-start | bytes 24584 | tf_op jit(solution)/shard_map/ppermute | solution.py:21
  397.3 6.3 %collective-permute-start.15 = (bf16[16,256]{1,0:T(8,128)(2,1)S(1)}, bf16[16,256]{1,0:T(8,128)(2,1)S(1)}, u32[]{:S(2)}, u32[]{:S(2)}) collective-permute-start(bf16[16,256]{1,0:T(8,128)(2,1)S(1)} %get-tuple-element.20), channel_id=1, source_target_pairs={{0,28},{4,0},{8,4},{12,8},{16,12},{20,16},{24,20},{28,24},{1,29},{... | collective-permute-start | bytes 24584 | tf_op jit(solution)/shard_map/ppermute | solution.py:24
  403.6 6.3 %collective-permute-start.16 = (bf16[16,256]{1,0:T(8,128)(2,1)S(1)}, bf16[16,256]{1,0:T(8,128)(2,1)S(1)}, u32[]{:S(2)}, u32[]{:S(2)}) collective-permute-start(bf16[16,256]{1,0:T(8,128)(2,1)S(1)} %collective-permute-done.14), channel_id=1, source_target_pairs={{0,4},{4,8},{8,12},{12,16},{16,20},{20,24},{24,28},{28,0},{1,5},{5... | collective-permute-start | bytes 24584 | tf_op jit(solution)/shard_map/ppermute | solution.py:21
  403.6 6.3 %collective-permute-start.17 = (bf16[16,256]{1,0:T(8,128)(2,1)S(1)}, bf16[16,256]{1,0:T(8,128)(2,1)S(1)}, u32[]{:S(2)}, u32[]{:S(2)}) collective-permute-start(bf16[16,256]{1,0:T(8,128)(2,1)S(1)} %collective-permute-done.15), channel_id=1, source_target_pairs={{0,28},{4,0},{8,4},{12,8},{16,12},{20,16},{24,20},{28,24},{1,29},{... | collective-permute-start | bytes 24584 | tf_op jit(solution)/shard_map/ppermute | solution.py:24
  410.0 6.3 %collective-permute-start.18 = (bf16[16,256]{1,0:T(8,128)(2,1)S(1)}, bf16[16,256]{1,0:T(8,128)(2,1)S(1)}, u32[]{:S(2)}, u32[]{:S(2)}) collective-permute-start(bf16[16,256]{1,0:T(8,128)(2,1)S(1)} %collective-permute-done.16), channel_id=1, source_target_pairs={{0,4},{4,8},{8,12},{12,16},{16,20},{20,24},{24,28},{28,0},{1,5},{5... | collective-permute-start | bytes 24584 | tf_op jit(solution)/shard_map/ppermute | solution.py:21
  410.0 6.3 %collective-permute-start.19 = (bf16[16,256]{1,0:T(8,128)(2,1)S(1)}, bf16[16,256]{1,0:T(8,128)(2,1)S(1)}, u32[]{:S(2)}, u32[]{:S(2)}) collective-permute-start(bf16[16,256]{1,0:T(8,128)(2,1)S(1)} %collective-permute-done.17), channel_id=1, source_target_pairs={{0,28},{4,0},{8,4},{12,8},{16,12},{20,16},{24,20},{28,24},{1,29},{... | collective-permute-start | bytes 24584 | tf_op jit(solution)/shard_map/ppermute | solution.py:24
  416.3 6.3 %collective-permute-start.20 = (bf16[16,256]{1,0:T(8,128)(2,1)S(1)}, bf16[16,256]{1,0:T(8,128)(2,1)S(1)}, u32[]{:S(2)}, u32[]{:S(2)}) collective-permute-start(bf16[16,256]{1,0:T(8,128)(2,1)S(1)} %collective-permute-done.18), channel_id=1, source_target_pairs={{0,4},{4,8},{8,12},{12,16},{16,20},{20,24},{24,28},{28,0},{1,5},{5... | collective-permute-start | bytes 24584 | tf_op jit(solution)/shard_map/ppermute | solution.py:21
  422.8 84.0 %copy-start.3 = (bf16[1,16,64,128]{3,2,1,0:T(8,128)(2,1)S(1)}, bf16[1,16,64,128]{3,2,1,0:T(8,128)(2,1)}, u32[]{:S(2)}) copy-start(bf16[1,16,64,128]{3,2,1,0:T(8,128)(2,1)} %get-tuple-element.25) | copy-start | bytes 786436
  422.8 84.0 %copy-start.4 = (bf16[1,16,64,128]{3,2,1,0:T(8,128)(2,1)S(1)}, bf16[1,16,64,128]{3,2,1,0:T(8,128)(2,1)}, u32[]{:S(2)}) copy-start(bf16[1,16,64,128]{3,2,1,0:T(8,128)(2,1)} %get-tuple-element.26) | copy-start | bytes 786436
  422.9 84.0 %copy-start.5 = (bf16[1,16,64,128]{3,2,1,0:T(8,128)(2,1)S(1)}, bf16[1,16,64,128]{3,2,1,0:T(8,128)(2,1)}, u32[]{:S(2)}) copy-start(bf16[1,16,64,128]{3,2,1,0:T(8,128)(2,1)} %get-tuple-element.40) | copy-start | bytes 786436
  422.9 84.0 %copy-start.6 = (bf16[1,16,64,128]{3,2,1,0:T(8,128)(2,1)S(1)}, bf16[1,16,64,128]{3,2,1,0:T(8,128)(2,1)}, u32[]{:S(2)}) copy-start(bf16[1,16,64,128]{3,2,1,0:T(8,128)(2,1)} %get-tuple-element.41) | copy-start | bytes 786436
  506.0 6.4 %collective-permute-start.21 = (bf16[16,256]{1,0:T(8,128)(2,1)S(1)}, bf16[16,256]{1,0:T(8,128)(2,1)S(1)}, u32[]{:S(2)}, u32[]{:S(2)}) collective-permute-start(bf16[16,256]{1,0:T(8,128)(2,1)S(1)} %get-tuple-element.18), channel_id=1, source_target_pairs={{0,4},{4,8},{8,12},{12,16},{16,20},{20,24},{24,28},{28,0},{1,5},{5... | collective-permute-start | bytes 24584 | tf_op jit(solution)/shard_map/ppermute | solution.py:21
  507.9 5.3 collective-permute-start.22
  512.4 6.3 %collective-permute-start.23 = (bf16[16,256]{1,0:T(8,128)(2,1)S(1)}, bf16[16,256]{1,0:T(8,128)(2,1)S(1)}, u32[]{:S(2)}, u32[]{:S(2)}) collective-permute-start(bf16[16,256]{1,0:T(8,128)(2,1)S(1)} %collective-permute-done.21), channel_id=1, source_target_pairs={{0,4},{4,8},{8,12},{12,16},{16,20},{20,24},{24,28},{28,0},{1,5},{5... | collective-permute-start | bytes 24584 | tf_op jit(solution)/shard_map/ppermute | solution.py:21
  513.2 6.3 %collective-permute-start.24 = (bf16[16,256]{1,0:T(8,128)(2,1)S(1)}, bf16[16,256]{1,0:T(8,128)(2,1)S(1)}, u32[]{:S(2)}, u32[]{:S(2)}) collective-permute-start(bf16[16,256]{1,0:T(8,128)(2,1)S(1)} %collective-permute-done.22), channel_id=1, source_target_pairs={{0,28},{4,0},{8,4},{12,8},{16,12},{20,16},{24,20},{28,24},{1,29},{... | collective-permute-start | bytes 24584 | tf_op jit(solution)/shard_map/ppermute | solution.py:24
  518.8 6.3 %collective-permute-start.25 = (bf16[16,256]{1,0:T(8,128)(2,1)S(1)}, bf16[16,256]{1,0:T(8,128)(2,1)S(1)}, u32[]{:S(2)}, u32[]{:S(2)}) collective-permute-start(bf16[16,256]{1,0:T(8,128)(2,1)S(1)} %collective-permute-done.23), channel_id=1, source_target_pairs={{0,4},{4,8},{8,12},{12,16},{16,20},{20,24},{24,28},{28,0},{1,5},{5... | collective-permute-start | bytes 24584 | tf_op jit(solution)/shard_map/ppermute | solution.py:21
  519.6 6.3 %collective-permute-start.26 = (bf16[16,256]{1,0:T(8,128)(2,1)S(1)}, bf16[16,256]{1,0:T(8,128)(2,1)S(1)}, u32[]{:S(2)}, u32[]{:S(2)}) collective-permute-start(bf16[16,256]{1,0:T(8,128)(2,1)S(1)} %collective-permute-done.24), channel_id=1, source_target_pairs={{0,28},{4,0},{8,4},{12,8},{16,12},{20,16},{24,20},{28,24},{1,29},{... | collective-permute-start | bytes 24584 | tf_op jit(solution)/shard_map/ppermute | solution.py:24
  525.1 6.3 %collective-permute-start.27 = (bf16[16,256]{1,0:T(8,128)(2,1)S(1)}, bf16[16,256]{1,0:T(8,128)(2,1)S(1)}, u32[]{:S(2)}, u32[]{:S(2)}) collective-permute-start(bf16[16,256]{1,0:T(8,128)(2,1)S(1)} %collective-permute-done.25), channel_id=1, source_target_pairs={{0,4},{4,8},{8,12},{12,16},{16,20},{20,24},{24,28},{28,0},{1,5},{5... | collective-permute-start | bytes 24584 | tf_op jit(solution)/shard_map/ppermute | solution.py:21
  531.5 0.6 copy-start.9
Sparse Core Ops, SparseCore 0:
  165.8 68.1 all-reduce.10
  426.1 68.0 all-reduce.8
